TPU v7x, 128 devices: a whole 4x4x4 slice. The times are simulated.
128 devices in a mesh: tm: 32 (over x, z, core), tp: 4 (over y).
Axes of the slice: x: 4, y: 4, z: 4, core: 2. Of those that a mesh axis runs over, the one named last changes fastest.
Arguments:
- trajectory: float32 [64, 128, 3072], P('tm', None, 'tp'), may hold values from -6 to 6
- offset: int32 [1], replicated, may hold values from 0 to 63
- step_gaps: int32 [64], P('tm'), may hold values from 1 to 4, as said below
- qkv_weight: bfloat16 [3072, 3, 3072], P(None, None, 'tp')
- out_weight: bfloat16 [3072, 3072], P('tp'), may hold values from -4 to 4
- mod_weight: bfloat16 [256, 3, 3072], P(None, None, 'tp'), may hold values from -0.375 to 0.375
Outputs:
- advanced: float32 [64, 128, 3072], P('tm', None, 'tp')
Inputs may be any that keep to these rules, and one draw needn't show every extreme that they name: `step_gaps`: in aligned blocks of 2 timesteps, the gaps of block b sum to an even number for even b and to an odd number for odd b.
All inputs are finite; a program needn't handle non-finite values.
Results may differ from a plain program's by a relative error of at most 0.007.
Values may be sent and summed in bfloat16 or wider, within the bound.
No kernel may reach another device: no remote copies, remote signals or barrier semaphores. Data moves between devices by JAX's collectives and lax.ppermute only.
A program may use at most 128 MiB of HBM per device.

v0:
```python
import math
import jax
import jax.numpy as jnp
from jax import lax
from jax.sharding import PartitionSpec as P

HD = 128
FREQ = 256
ITERS = 2


def prefix(array, axis, combine, identity):
    size, place = (lax.axis_size(axis), lax.axis_index(axis))
    everything = lax.all_gather(array, axis)
    start = jnp.broadcast_to(jnp.asarray(identity, array.dtype), array.shape)

    def turn(k, before):
        reached = k < place
        new = combine(before, everything[k])
        return jnp.where(reached, new, before)

    return lax.fori_loop(0, size, turn, start)


def broadcast(block, axis, holder):
    block = jnp.where(lax.axis_index(axis) == holder, block, jnp.zeros_like(block))
    return lax.psum(block, axis)


def prefix_2(array, axis, join, neutral):
    place = lax.axis_index(axis)
    gathered = lax.all_gather(array.astype(jnp.bfloat16), axis)
    state = jnp.zeros_like(array) + jnp.asarray(neutral, array.dtype)

    def one(turn, state):
        return join(state, lax.dynamic_index_in_dim(gathered, turn, 0, False).astype(array.dtype))

    return lax.fori_loop(0, place, one, state)


def add_up(earlier, later):
    return earlier + later


def embedding(sigma):
    half_freq = FREQ // 2
    frequencies = jnp.exp(-math.log(10000.0) * jnp.arange(half_freq, dtype=jnp.float32) / half_freq)
    angles = 1000.0 * sigma[:, None] * frequencies[None, :]
    return jnp.concatenate([jnp.cos(angles), jnp.sin(angles)], -1).astype(jnp.bfloat16)


def body(trajectory, offset, step_gaps, qkv_weight, out_weight, mod_weight):
    steps_here, tok_count, col_count = trajectory.shape
    full_width = qkv_weight.shape[0]
    time_count = steps_here * lax.axis_size("tm")
    level_count = 5 * time_count
    before = prefix(jnp.sum(step_gaps), "tm", add_up, jnp.int32(0))
    levels = (offset[0] + before + jnp.cumsum(step_gaps) - step_gaps).astype(jnp.float32)
    sigma = 1.0 - levels / level_count
    step_size = step_gaps.astype(jnp.float32) / level_count
    embed_rows = embedding(sigma)
    full_mod = lax.all_gather(mod_weight, "tp", axis=2, tiled=True)
    modulation = jnp.dot(
        embed_rows, full_mod.reshape(FREQ, 3 * full_width), preferred_element_type=jnp.float32
    ).reshape(steps_here, 3, full_width)
    gate_rows = lax.dynamic_slice_in_dim(
        modulation[:, 2], lax.axis_index("tp") * col_count, col_count, 1
    )
    base_point = broadcast(trajectory[0], "tm", 0)
    flat_qkv = qkv_weight.reshape(full_width, -1)
    states = trajectory
    points = trajectory
    for sweep in range(ITERS):
        whole_rows = lax.all_gather(states, "tp", axis=2, tiled=True)
        row_mean = jnp.sum(whole_rows, -1, keepdims=True) / full_width
        variance = (
            jnp.sum(whole_rows * whole_rows, -1, keepdims=True) / full_width - row_mean * row_mean
        )
        inv_std = lax.rsqrt(variance + 1e-06)
        normed = (
            (whole_rows - row_mean) * inv_std * (1.0 + modulation[:, 1][:, None, :])
            + modulation[:, 0][:, None, :]
        ).astype(jnp.bfloat16)
        projected = jnp.einsum("std,de->ste", normed, flat_qkv, preferred_element_type=jnp.float32)
        projected = projected.astype(jnp.bfloat16).reshape(steps_here, tok_count, 3, -1, HD)
        queries = projected[:, :, 0]
        key_rows = projected[:, :, 1]
        values = projected[:, :, 2]
        scores = jnp.einsum(
            "sqhd,skhd->shqk", queries, key_rows, preferred_element_type=jnp.float32
        ) * (1.0 / math.sqrt(HD))
        row_max = jnp.max(scores, -1, keepdims=True)
        weights_exp = jnp.exp(scores - row_max)
        probs = (weights_exp / jnp.sum(weights_exp, -1, keepdims=True)).astype(jnp.bfloat16)
        attended = jnp.einsum(
            "shqk,skhd->sqhd", probs, values, preferred_element_type=jnp.float32
        ).astype(jnp.bfloat16)
        attended = attended.reshape(steps_here, tok_count, -1)
        head_out = jnp.einsum(
            "sqe,ed->sqd", attended, out_weight, preferred_element_type=jnp.float32
        )
        col_share = lax.psum_scatter(
            head_out.astype(jnp.bfloat16), "tp", scatter_dimension=2, tiled=True
        ).astype(jnp.float32)
        drifts = gate_rows[:, None, :] * col_share
        increments = -step_size[:, None, None] * drifts
        local_cum = jnp.cumsum(increments, 0)
        prefix_sum = prefix_2(
            local_cum[-1], "tm", add_up, jnp.zeros((tok_count, col_count), jnp.float32)
        )
        entry_point = prefix_sum + base_point
        points = entry_point[None] + local_cum
        states = jnp.concatenate([entry_point[None], points[:-1]], 0)
    return points


def solution(mesh):
    placed = (
        P("tm", None, "tp"),
        P(),
        P("tm"),
        P(None, None, "tp"),
        P("tp", None),
        P(None, None, "tp"),
    )
    return jax.shard_map(
        body, mesh=mesh, in_specs=placed, out_specs=P("tm", None, "tp"), check_vma=False
    )
```

profile of v0, /device:TPU:103, one launch (start us, length us, event | category | flops | bytes accessed | tf_op | source)
XLA Modules:
  0.0 483.2 jit_solution(12489201418532556773)
XLA Ops:
  7.3 2.4 copy.33
  11.3 18.7 %copy.34 = bf16[3072,3,768]{0,2,1:T(8,128)(2,1)} copy(bf16[3072,3,768]{2,0,1:T(8,128)(2,1)} %param.15) | data formatting | bytes 28311552 | tf_op args[3]
  30.7 1.4 dynamic-update-slice
  32.0 8.7 %all-reduce = s32[32]{0:T(128)S(1)} all-reduce(s32[32]{0:T(128)S(1)} %dynamic-update-slice), channel_id=1, replica_groups=mesh['tm'=32,'tp'=4] {'tm'}, use_global_device_ids=true, to_apply=%add | all-reduce | flops 32 | bytes 256
  40.7 40.6 %while.33 = (s32[]{:T(128)}, s32[]{:T(128)}, s32[]{:T(128)}, s32[32]{0:T(128)S(1)}, s32[]{:T(128)}) while((s32[]{:T(128)}, s32[]{:T(128)}, s32[]{:T(128)}, s32[32]{0:T(128)S(1)}, s32[]{:T(128)}) %tuple.62), condition=%wide.region_2.3_spmd, body=%wide.region_1.2_spmd.sunk | while | flops 5 | bytes 107 | solution.py:22
  81.5 2.5 fusion.55
  84.0 20.4 %all-gather.6.cloned.1.call-done = bf16[256,3,3072]{0,2,1:T(8,128)(2,1)} async-done(((bf16[256,3,768]{0,2,1:T(8,128)(2,1)}), bf16[256,3,3072]{0,2,1:T(8,128)(2,1)}) %all-gather.6.cloned.1.call-update) | async-done | bytes 4718608 | tf_op jit(solution)/shard_map/all_gather | solution.py:62
  104.4 3.6 fusion.2
  108.1 10.1 %convolution_convert_fusion.1 = bf16[2,128,2304]{2,1,0:T(8,128)(2,1)} fusion(bf16[3072,2304,1]{0,1,2:T(8,128)(2,1)} %bitcast.116, f32[2,128,3072]{2,1,0:T(8,128)S(1)} %copy-done, f32[2,3072]{1,0:T(2,128)S(1)} %get-tuple-element.162, f32[2,3072]{1,0:T(2,128)S(1)} %get-tuple-element.163, f32[2,128]{1,0:T(2,128)S(1)} %get-tuple-element.167, ...), kind=kOutput, calls=%fused_computation.13 | convolution fusion | flops 3628400640 | bytes 18532352 | tf_op jit(solution)/shard_map/std,de->ste/dot_general | solution.py:84
  118.2 1.7 copy.36
  121.0 4.9 %fusion.8 = bf16[2,128,3072]{2,1,0:T(8,128)(2,1)} fusion(bf16[2,128,768]{1,2,0:T(8,128)(2,1)S(1)} %bitcast.125, bf16[768,3072]{1,0:T(8,128)(2,1)} %param.16), kind=kOutput, calls=%fused_computation.10 | convolution fusion | flops 1208745984 | bytes 6684672 | tf_op jit(solution)/shard_map/sqe,ed->sqd/dot_general | solution.py:99
  126.0 25.2 %reduce-scatter.3.cloned.1.call-done = bf16[2,128,768]{2,1,0:T(8,128)(2,1)} async-done(((bf16[2,128,3072]{2,1,0:T(8,128)(2,1)}), bf16[2,128,768]{2,1,0:T(8,128)(2,1)}) %reduce-scatter.3.cloned.1.call-update) | async-done | bytes 393232 | tf_op jit(solution)/shard_map/reduce_scatter | solution.py:102
  151.2 1.1 fusion.30
  154.0 47.3 %all-gather.10.cloned.1.call-done = bf16[32,128,768]{2,1,0:T(8,128)(2,1)} async-done(((bf16[1,128,768]{2,1,0:T(8,128)(2,1)}), bf16[32,128,768]{2,1,0:T(8,128)(2,1)}) %all-gather.10.cloned.1.call-update) | async-done | bytes 6291472 | tf_op jit(solution)/shard_map/all_gather | solution.py:32
  201.3 31.9 %while.34 = (s32[]{:T(128)}, f32[128,768]{1,0:T(8,128)S(1)}, s32[]{:T(128)}, bf16[32,128,768]{2,1,0:T(8,128)(2,1)}, s32[]{:T(128)}, /*index=5*/s32[]{:T(128)}, s32[]{:T(128)}) while((s32[]{:T(128)}, f32[128,768]{1,0:T(8,128)S(1)}, s32[]{:T(128)}, bf16[32,128,768]{2,1,0:T(8,128)(2,1)}, s32[]{:T(128)}, /*index=5*/s32[]{:T(128)}, ...), condition=%wide.region_11.12_spmd, body=%wide.region_10.11_spmd.sunk | while | flops 196613 | bytes 983155 | solution.py:38
  213.7 1.0 convert_add_fusion.4
  215.7 1.0 convert_add_fusion.4
  218.8 1.0 convert_add_fusion.4
  219.9 1.0 convert_add_fusion.4
  220.9 1.0 convert_add_fusion.4
  221.9 1.0 convert_add_fusion.4
  225.0 1.0 convert_add_fusion.4
  233.2 73.6 %all-reduce.3.cloned.1.call-done = f32[128,768]{1,0:T(8,128)} async-done(((f32[128,768]{1,0:T(8,128)}), f32[128,768]{1,0:T(8,128)}) %all-reduce.3.cloned.1.call-update) | async-done | bytes 393232 | tf_op jit(solution)/shard_map/psum | solution.py:27
  306.8 1.0 add.136
  309.1 40.2 %all-gather.12.cloned.1.call-done = f32[2,128,3072]{2,1,0:T(8,128)} async-done(((f32[2,128,768]{2,1,0:T(8,128)}), f32[2,128,3072]{2,1,0:T(8,128)}) %all-gather.12.cloned.1.call-update) | async-done | bytes 3145744 | tf_op jit(solution)/shard_map/all_gather | solution.py:74
  349.3 2.6 fusion.54
  352.1 9.1 %convolution_convert_fusion = bf16[2,128,2304]{2,1,0:T(8,128)(2,1)S(1)} fusion(bf16[3072,2304,1]{0,1,2:T(8,128)(2,1)} %bitcast.117, f32[2,128,3072]{2,1,0:T(8,128)S(1)} %copy-done.1, f32[2,128]{1,0:T(2,128)S(1)} %get-tuple-element.165, f32[2,128]{1,0:T(2,128)S(1)} %get-tuple-element.164, f32[2,3072]{1,0:T(2,128)S(1)} %get-tuple-element.162, ...), kind=kOutput, calls=%fused_computation.12 | convolution fusion | flops 3628400640 | bytes 18532352 | tf_op jit(solution)/shard_map/std,de->ste/dot_general | solution.py:84
  363.1 4.9 %fusion.11 = bf16[2,128,3072]{2,1,0:T(8,128)(2,1)} fusion(bf16[2,128,768]{1,2,0:T(8,128)(2,1)S(1)} %bitcast.126, bf16[768,3072]{1,0:T(8,128)(2,1)} %param.16), kind=kOutput, calls=%fused_computation.11 | convolution fusion | flops 1208745984 | bytes 6684672 | tf_op jit(solution)/shard_map/sqe,ed->sqd/dot_general | solution.py:99
  368.1 25.1 %reduce-scatter.5.cloned.1.call-done = bf16[2,128,768]{2,1,0:T(8,128)(2,1)} async-done(((bf16[2,128,3072]{2,1,0:T(8,128)(2,1)}), bf16[2,128,768]{2,1,0:T(8,128)(2,1)}) %reduce-scatter.5.cloned.1.call-update) | async-done | bytes 393232 | tf_op jit(solution)/shard_map/reduce_scatter | solution.py:102
  393.2 1.1 fusion.26
  395.0 48.4 %all-gather.14.cloned.1.call-done = bf16[32,128,768]{2,1,0:T(8,128)(2,1)} async-done(((bf16[1,128,768]{2,1,0:T(8,128)(2,1)}), bf16[32,128,768]{2,1,0:T(8,128)(2,1)}) %all-gather.14.cloned.1.call-update) | async-done | bytes 6291472 | tf_op jit(solution)/shard_map/all_gather | solution.py:32
  443.5 31.9 %while.35 = (s32[]{:T(128)}, f32[128,768]{1,0:T(8,128)S(1)}, s32[]{:T(128)}, bf16[32,128,768]{2,1,0:T(8,128)(2,1)}, s32[]{:T(128)}, /*index=5*/s32[]{:T(128)}, s32[]{:T(128)}) while((s32[]{:T(128)}, f32[128,768]{1,0:T(8,128)S(1)}, s32[]{:T(128)}, bf16[32,128,768]{2,1,0:T(8,128)(2,1)}, s32[]{:T(128)}, /*index=5*/s32[]{:T(128)}, ...), condition=%wide.region_20.21_spmd, body=%wide.region_19.20_spmd.sunk | while | flops 196613 | bytes 983155 | solution.py:38
  (143 shorter events, 84.9 us)
Async XLA Ops:
  6.5 3.3 copy-start.4
  6.5 75.0 %all-gather.8.cloned.1.call-start = ((), (), s32[]{:S(2)}) async-start(), calls=%async_computation.3 | async-start | bytes 3932160 | tf_op jit(solution)/shard_map/all_gather | solution.py:74
  7.3 97.2 %all-gather.6.cloned.1.call-start = ((), (), s32[]{:S(2)}) async-start(), calls=%async_computation.2 | async-start | bytes 5898240 | tf_op jit(solution)/shard_map/all_gather | solution.py:62
  9.7 141.5 %reduce-scatter.3.cloned.1.call-start = ((), (), s32[]{:S(2)}) async-start(), calls=%async_computation.4 | async-start | bytes 1966080 | tf_op jit(solution)/shard_map/reduce_scatter | solution.py:102
  11.3 18.7 %copy-start.5 = (u32[128]{0:T(128)S(1)}, u32[128]{0:T(128)}, u32[]{:S(2)}) copy-start(u32[128]{0:T(128)} %constant.91) | copy-start | bytes 1540
  84.0 24.1 %copy-start = (f32[2,128,3072]{2,1,0:T(8,128)S(1)}, f32[2,128,3072]{2,1,0:T(8,128)}, u32[]{:S(2)}) copy-start(f32[2,128,3072]{2,1,0:T(8,128)} %all-gather.8.cloned.1.call-done) | copy-start | bytes 9437188
  125.9 27.2 %copy-start.2 = (f32[2,128,768]{2,1,0:T(8,128)S(1)}, f32[2,128,768]{2,1,0:T(8,128)}, u32[]{:S(2)}) copy-start(f32[2,128,768]{2,1,0:T(8,128)} %param.12) | copy-start | bytes 2359300
  125.9 75.4 %all-gather.10.cloned.1.call-start = ((), (), s32[]{:S(2)}) async-start(), calls=%async_computation.5 | async-start | bytes 6488064 | tf_op jit(solution)/shard_map/all_gather | solution.py:32
  153.0 153.8 %all-reduce.3.cloned.1.call-start = ((), (), s32[]{:S(2)}) async-start(), calls=%async_computation.6 | async-start | bytes 786432 | tf_op jit(solution)/shard_map/psum | solution.py:27
  153.9 195.4 %all-gather.12.cloned.1.call-start = ((), (), s32[]{:S(2)}) async-start(), calls=%async_computation.7 | async-start | bytes 3932160 | tf_op jit(solution)/shard_map/all_gather | solution.py:74
  308.9 84.3 %reduce-scatter.5.cloned.1.call-start = ((), (), s32[]{:S(2)}) async-start(), calls=%async_computation.8 | async-start | bytes 1966080 | tf_op jit(solution)/shard_map/reduce_scatter | solution.py:102
  349.3 2.8 copy-start.1
  368.1 75.4 %all-gather.14.cloned.1.call-start = ((), (), s32[]{:S(2)}) async-start(), calls=%async_computation.9 | async-start | bytes 6488064 | tf_op jit(solution)/shard_map/all_gather | solution.py:32
  394.3 81.1 %copy-start.3 = (f32[128,768]{1,0:T(8,128)S(1)}, f32[128,768]{1,0:T(8,128)}, u32[]{:S(2)}) copy-start(f32[128,768]{1,0:T(8,128)} %all-reduce.3.cloned.1.call-done) | copy-start | bytes 1179652
Sparse Core Ops, SparseCore 0:
  9.0 40.7 all-gather.7
  51.5 52.8 all-gather.5
  126.0 25.1 reduce-scatter.2
  153.3 47.9 all-gather.9
  204.4 102.4 all-reduce.2
  309.0 40.2 all-gather.11
  368.2 24.9 reduce-scatter.4
  395.4 47.9 all-gather.13
where the time goes:
time: 486 us; the launch traced here: 483 us
  waiting for transfers between devices  281 us (58%)
  other arithmetic  74.2 us (15%)
  local copies, waits for them, and re-layouts  46.7 us (10%)
  matrix products  34.9 us (7%)
  loops' own time  22.8 us (5%)
  between operations  14.4 us (3%)
  blocking collectives  8.69 us (2%)
    all_gather x2, waiting for transfers between devices, prefix_2(): gathered = lax.all_gather(array.astype(jnp.bfloat16), axis)  95.7 us
    psum x1, waiting for transfers between devices, broadcast(): return lax.psum(block, axis)  73.6 us
    add x62, other arithmetic, add_up(): return earlier + later  62.1 us
    reduce_scatter x2, waiting for transfers between devices, body(): lax.psum_scatter(head_out.astype(jnp.bfloat16), 'tp', scatter_dimension=2...  50.3 us
    all_gather x2, waiting for transfers between devices, body(): whole_rows = lax.all_gather(states, 'tp', axis=2, tiled=True)  40.2 us
    unnamed x17, local copies, waits for them, and re-layouts  23.4 us
    another operation x1, loops' own time, prefix(): return lax.fori_loop(0, size, turn, start)  21.1 us
    all_gather x1, waiting for transfers between devices, body(): full_mod = lax.all_gather(mod_weight, 'tp', axis=2, tiled=True)  20.4 us
  transfers between devices with their start and end apart: 8, of which 7 were waited for; matrix products, arithmetic and copies ran while one was open for 16% of the time, Pallas kernels for 0%

commit v1 on v0

--- a/solution.py
+++ b/solution.py
@@ -7,6 +7,24 @@
 HD = 128
 FREQ = 256
 ITERS = 2
+
+
+def ring_gather(value, axis, dim):
+    ways, here, turn = (lax.axis_size(axis), lax.axis_index(axis), value.shape[dim])
+    dims = [n * ways if d == dim else n for d, n in enumerate(value.shape)]
+    full = lax.dynamic_update_slice_in_dim(
+        jnp.zeros(dims, value.dtype), value, here * turn, axis=dim
+    )
+    going_up = going_down = value
+    for far in range(1, ways // 2 + 1):
+        going_up = lax.ppermute(going_up, axis, [(d, (d + 1) % ways) for d in range(ways)])
+        full = lax.dynamic_update_slice_in_dim(full, going_up, (here - far) % ways * turn, axis=dim)
+        if 2 * far < ways:
+            going_down = lax.ppermute(going_down, axis, [(d, (d - 1) % ways) for d in range(ways)])
+            full = lax.dynamic_update_slice_in_dim(
+                full, going_down, (here + far) % ways * turn, axis=dim
+            )
+    return full
 
 
 def prefix(array, axis, combine, identity):
@@ -59,7 +77,7 @@
     sigma = 1.0 - levels / level_count
     step_size = step_gaps.astype(jnp.float32) / level_count
     embed_rows = embedding(sigma)
-    full_mod = lax.all_gather(mod_weight, "tp", axis=2, tiled=True)
+    full_mod = ring_gather(mod_weight, "tp", 2)
     modulation = jnp.dot(
         embed_rows, full_mod.reshape(FREQ, 3 * full_width), preferred_element_type=jnp.float32
     ).reshape(steps_here, 3, full_width)

time: 486 us -> 507 us (1.043)
  waiting for transfers between devices: 281 us -> 304 us
    ppermute x0 -> x3, waiting for transfers between devices: none -> 38 us  [the longest x2 38 us: ring_gather(): lax.ppermute(going_up, axis, [(d, (d + 1) % ways) for d in range(ways)])]
    all_gather x1 -> x0, waiting for transfers between devices: 20.4 us -> none  [body(): full_mod = lax.all_gather(mod_weight, 'tp', axis=2, tiled=True)]
    reduce_scatter x2, waiting for transfers between devices: 50.3 us -> 55.6 us  [body(): lax.psum_scatter(head_out.astype(jnp.bfloat16), 'tp', scatter_dimension=2...]
  transfers between devices with their start and end apart: 8 -> 10, of which waited for: 7 -> 7; matrix products, arithmetic and copies ran while one was open for 16% -> 15% of each run, Pallas kernels for 0% -> 0%
where the time goes in v1:
time: 507 us; the launch traced here: 505 us
  waiting for transfers between devices  304 us (60%)
  other arithmetic  74.3 us (15%)
  local copies, waits for them, and re-layouts  45.3 us (9%)
  matrix products  31.6 us (6%)
  loops' own time  19.9 us (4%)
  between operations  14.4 us (3%)
  blocking collectives  10.7 us (2%)
    all_gather x2, waiting for transfers between devices, prefix_2(): gathered = lax.all_gather(array.astype(jnp.bfloat16), axis)  96 us
    psum x1, waiting for transfers between devices, broadcast(): return lax.psum(block, axis)  73.6 us
    add x62, other arithmetic, add_up(): return earlier + later  62.1 us
    reduce_scatter x2, waiting for transfers between devices, body(): lax.psum_scatter(head_out.astype(jnp.bfloat16), 'tp', scatter_dimension=2...  55.6 us
    all_gather x2, waiting for transfers between devices, body(): whole_rows = lax.all_gather(states, 'tp', axis=2, tiled=True)  40.2 us
    ppermute x2, waiting for transfers between devices, ring_gather(): lax.ppermute(going_up, axis, [(d, (d + 1) % ways) for d in range(ways)])  38 us
    unnamed x17, local copies, waits for them, and re-layouts  22.7 us
    dot_general x2, matrix products, body(): jnp.einsum('std,de->ste', normed, flat_qkv, preferred_element_type=jnp.fl...  18.2 us
  transfers between devices with their start and end apart: 10, of which 7 were waited for; matrix products, arithmetic and copies ran while one was open for 15% of the time, Pallas kernels for 0%

profile of v1, /device:TPU:103, one launch (start us, length us, event | category | flops | bytes accessed | tf_op | source)
XLA Modules:
  0.0 504.7 jit_solution(6879230840672959516)
XLA Ops:
  7.3 1.6 copy.35
  8.9 1.4 collective-permute-start
  10.2 1.5 collective-permute-start.1
  11.8 38.0 %collective-permute-done = bf16[256,3,768]{0,2,1:T(8,128)(2,1)S(1)} collective-permute-done((bf16[256,3,768]{0,2,1:T(8,128)(2,1)S(1)}, bf16[256,3,768]{0,2,1:T(8,128)(2,1)S(1)}, u32[]{:S(2)}, u32[]{:S(2)}) %collective-permute-start) | collective-permute-done | bytes 1179680 | tf_op jit(solution)/shard_map/ppermute | solution.py:20
  52.1 18.7 %copy.38 = bf16[3072,3,768]{0,2,1:T(8,128)(2,1)} copy(bf16[3072,3,768]{2,0,1:T(8,128)(2,1)} %param.15) | data formatting | bytes 28311552 | tf_op args[3]
  71.5 1.3 dynamic-update-slice
  72.8 10.7 %all-reduce = s32[32]{0:T(128)S(1)} all-reduce(s32[32]{0:T(128)S(1)} %dynamic-update-slice), channel_id=1, replica_groups=mesh['tm'=32,'tp'=4] {'tm'}, use_global_device_ids=true, to_apply=%add | all-reduce | flops 32 | bytes 256
  83.5 35.9 %while.33 = (s32[]{:T(128)}, s32[]{:T(128)}, s32[]{:T(128)}, s32[32]{0:T(128)S(1)}, s32[]{:T(128)}) while((s32[]{:T(128)}, s32[]{:T(128)}, s32[]{:T(128)}, s32[32]{0:T(128)S(1)}, s32[]{:T(128)}) %tuple.62), condition=%wide.region_2.3_spmd, body=%wide.region_1.2_spmd.sunk | while | flops 5 | bytes 107 | solution.py:40
  120.2 1.4 constant_dynamic-update-slice_fusion.1
  121.7 1.3 fusion.2
  123.0 2.6 fusion.55
  125.9 9.1 %convolution_convert_fusion.1 = bf16[2,128,2304]{2,1,0:T(8,128)(2,1)S(1)} fusion(bf16[3072,2304,1]{0,1,2:T(8,128)(2,1)} %bitcast.116, f32[2,128,3072]{2,1,0:T(8,128)S(1)} %copy-done, f32[2,3072]{1,0:T(2,128)S(1)} %get-tuple-element.162, f32[2,3072]{1,0:T(2,128)S(1)} %get-tuple-element.163, f32[2,128]{1,0:T(2,128)S(1)} %get-tuple-element.167, ...), kind=kOutput, calls=%fused_computation.13 | convolution fusion | flops 3628400640 | bytes 18532352 | tf_op jit(solution)/shard_map/std,de->ste/dot_general | solution.py:102
  136.9 4.9 fusion.8
  141.8 30.6 %reduce-scatter.3.cloned.1.call-done = bf16[2,128,768]{2,1,0:T(8,128)(2,1)} async-done(((bf16[2,128,3072]{2,1,0:T(8,128)(2,1)}), bf16[2,128,768]{2,1,0:T(8,128)(2,1)}) %reduce-scatter.3.cloned.1.call-update) | async-done | bytes 393232 | tf_op jit(solution)/shard_map/reduce_scatter | solution.py:120
  172.5 1.1 fusion.30
  175.2 47.5 %all-gather.7.cloned.1.call-done = bf16[32,128,768]{2,1,0:T(8,128)(2,1)} async-done(((bf16[1,128,768]{2,1,0:T(8,128)(2,1)}), bf16[32,128,768]{2,1,0:T(8,128)(2,1)}) %all-gather.7.cloned.1.call-update) | async-done | bytes 6291472 | tf_op jit(solution)/shard_map/all_gather | solution.py:50
  222.8 31.9 %while.34 = (s32[]{:T(128)}, f32[128,768]{1,0:T(8,128)S(1)}, s32[]{:T(128)}, bf16[32,128,768]{2,1,0:T(8,128)(2,1)}, s32[]{:T(128)}, /*index=5*/s32[]{:T(128)}, s32[]{:T(128)}) while((s32[]{:T(128)}, f32[128,768]{1,0:T(8,128)S(1)}, s32[]{:T(128)}, bf16[32,128,768]{2,1,0:T(8,128)(2,1)}, s32[]{:T(128)}, /*index=5*/s32[]{:T(128)}, ...), condition=%wide.region_11.12_spmd, body=%wide.region_10.11_spmd.sunk | while | flops 196613 | bytes 983155 | solution.py:56
  235.2 1.0 convert_add_fusion.4
  237.2 1.0 convert_add_fusion.4
  246.5 1.0 convert_add_fusion.4
  247.5 1.0 convert_add_fusion.4
  248.6 1.0 convert_add_fusion.4
  254.7 73.6 %all-reduce.3.cloned.1.call-done = f32[128,768]{1,0:T(8,128)} async-done(((f32[128,768]{1,0:T(8,128)}), f32[128,768]{1,0:T(8,128)}) %all-reduce.3.cloned.1.call-update) | async-done | bytes 393232 | tf_op jit(solution)/shard_map/psum | solution.py:45
  328.3 1.0 add.168
  330.6 40.2 %all-gather.9.cloned.1.call-done = f32[2,128,3072]{2,1,0:T(8,128)} async-done(((f32[2,128,768]{2,1,0:T(8,128)}), f32[2,128,3072]{2,1,0:T(8,128)}) %all-gather.9.cloned.1.call-update) | async-done | bytes 3145744 | tf_op jit(solution)/shard_map/all_gather | solution.py:92
  370.8 2.6 fusion.54
  373.6 9.1 %convolution_convert_fusion = bf16[2,128,2304]{2,1,0:T(8,128)(2,1)S(1)} fusion(bf16[3072,2304,1]{0,1,2:T(8,128)(2,1)} %bitcast.117, f32[2,128,3072]{2,1,0:T(8,128)S(1)} %copy-done.1, f32[2,128]{1,0:T(2,128)S(1)} %get-tuple-element.165, f32[2,128]{1,0:T(2,128)S(1)} %get-tuple-element.164, f32[2,3072]{1,0:T(2,128)S(1)} %get-tuple-element.162, ...), kind=kOutput, calls=%fused_computation.12 | convolution fusion | flops 3628400640 | bytes 18532352 | tf_op jit(solution)/shard_map/std,de->ste/dot_general | solution.py:102
  384.6 4.9 fusion.11
  389.6 25.0 %reduce-scatter.5.cloned.1.call-done = bf16[2,128,768]{2,1,0:T(8,128)(2,1)} async-done(((bf16[2,128,3072]{2,1,0:T(8,128)(2,1)}), bf16[2,128,768]{2,1,0:T(8,128)(2,1)}) %reduce-scatter.5.cloned.1.call-update) | async-done | bytes 393232 | tf_op jit(solution)/shard_map/reduce_scatter | solution.py:120
  414.6 1.1 fusion.26
  416.5 48.5 %all-gather.11.cloned.1.call-done = bf16[32,128,768]{2,1,0:T(8,128)(2,1)} async-done(((bf16[1,128,768]{2,1,0:T(8,128)(2,1)}), bf16[32,128,768]{2,1,0:T(8,128)(2,1)}) %all-gather.11.cloned.1.call-update) | async-done | bytes 6291472 | tf_op jit(solution)/shard_map/all_gather | solution.py:50
  465.0 31.9 %while.35 = (s32[]{:T(128)}, f32[128,768]{1,0:T(8,128)S(1)}, s32[]{:T(128)}, bf16[32,128,768]{2,1,0:T(8,128)(2,1)}, s32[]{:T(128)}, /*index=5*/s32[]{:T(128)}, s32[]{:T(128)}) while((s32[]{:T(128)}, f32[128,768]{1,0:T(8,128)S(1)}, s32[]{:T(128)}, bf16[32,128,768]{2,1,0:T(8,128)(2,1)}, s32[]{:T(128)}, /*index=5*/s32[]{:T(128)}, ...), condition=%wide.region_20.21_spmd, body=%wide.region_19.20_spmd.sunk | while | flops 196613 | bytes 983155 | solution.py:56
  (151 shorter events, 87.6 us)
Async XLA Ops:
  6.5 44.2 %copy-start.4 = (s32[2]{0:T(128)S(1)}, s32[2]{0:T(128)}, u32[]{:S(2)}) copy-start(s32[2]{0:T(128)} %param.14) | copy-start | bytes 28
  6.5 116.5 %all-gather.5.cloned.1.call-start = ((), (), s32[]{:S(2)}) async-start(), calls=%async_computation.2 | async-start | bytes 3932160 | tf_op jit(solution)/shard_map/all_gather | solution.py:92
  7.3 165.2 %reduce-scatter.3.cloned.1.call-start = ((), (), s32[]{:S(2)}) async-start(), calls=%async_computation.3 | async-start | bytes 1966080 | tf_op jit(solution)/shard_map/reduce_scatter | solution.py:120
  8.9 40.9 %collective-permute-start = (bf16[256,3,768]{0,2,1:T(8,128)(2,1)S(1)}, bf16[256,3,768]{0,2,1:T(8,128)(2,1)S(1)}, u32[]{:S(2)}, u32[]{:S(2)}) collective-permute-start(bf16[256,3,768]{0,2,1:T(8,128)(2,1)S(1)} %copy.35), channel_id=1, source_target_pairs={{0,1},{1,2},{2,3},{3,0},{4,5},{5,6},{6,7},{7,4},{8,9},{9,10},{10,1... | collective-permute-start | bytes 3538952 | tf_op jit(solution)/shard_map/ppermute | solution.py:20
  10.2 109.9 %collective-permute-start.1 = (bf16[256,3,768]{0,2,1:T(8,128)(2,1)S(1)}, bf16[256,3,768]{0,2,1:T(8,128)(2,1)}, u32[]{:S(2)}, u32[]{:S(2)}) collective-permute-start(bf16[256,3,768]{0,2,1:T(8,128)(2,1)S(1)} %copy.35), channel_id=1, source_target_pairs={{0,3},{1,0},{2,1},{3,2},{4,7},{5,4},{6,5},{7,6},{8,11},{9,8},{10,9... | collective-permute-start | bytes 3538952 | tf_op jit(solution)/shard_map/ppermute | solution.py:23
  49.8 71.7 %collective-permute-start.2 = (bf16[256,3,768]{0,2,1:T(8,128)(2,1)S(1)}, bf16[256,3,768]{0,2,1:T(8,128)(2,1)S(1)}, u32[]{:S(2)}, u32[]{:S(2)}) collective-permute-start(bf16[256,3,768]{0,2,1:T(8,128)(2,1)S(1)} %collective-permute-done), channel_id=1, source_target_pairs={{0,1},{1,2},{2,3},{3,0},{4,5},{5,6},{6,7},{7,4},{8,9},{9,10},{10,1... | collective-permute-start | bytes 3538952 | tf_op jit(solution)/shard_map/ppermute | solution.py:20
  52.1 18.7 %copy-start.5 = (u32[128]{0:T(128)S(1)}, u32[128]{0:T(128)}, u32[]{:S(2)}) copy-start(u32[128]{0:T(128)} %constant.120) | copy-start | bytes 1540
  123.0 2.8 copy-start
  141.8 32.6 %copy-start.2 = (f32[2,128,768]{2,1,0:T(8,128)S(1)}, f32[2,128,768]{2,1,0:T(8,128)}, u32[]{:S(2)}) copy-start(f32[2,128,768]{2,1,0:T(8,128)} %param.12) | copy-start | bytes 2359300
  141.8 81.0 %all-gather.7.cloned.1.call-start = ((), (), s32[]{:S(2)}) async-start(), calls=%async_computation.4 | async-start | bytes 6488064 | tf_op jit(solution)/shard_map/all_gather | solution.py:50
  174.3 154.0 %all-reduce.3.cloned.1.call-start = ((), (), s32[]{:S(2)}) async-start(), calls=%async_computation.5 | async-start | bytes 786432 | tf_op jit(solution)/shard_map/psum | solution.py:45
  175.2 195.6 %all-gather.9.cloned.1.call-start = ((), (), s32[]{:S(2)}) async-start(), calls=%async_computation.6 | async-start | bytes 3932160 | tf_op jit(solution)/shard_map/all_gather | solution.py:92
  330.4 84.2 %reduce-scatter.5.cloned.1.call-start = ((), (), s32[]{:S(2)}) async-start(), calls=%async_computation.7 | async-start | bytes 1966080 | tf_op jit(solution)/shard_map/reduce_scatter | solution.py:120
  370.8 2.8 copy-start.1
  389.6 75.4 %all-gather.11.cloned.1.call-start = ((), (), s32[]{:S(2)}) async-start(), calls=%async_computation.8 | async-start | bytes 6488064 | tf_op jit(solution)/shard_map/all_gather | solution.py:50
  415.7 81.1 %copy-start.3 = (f32[128,768]{1,0:T(8,128)S(1)}, f32[128,768]{1,0:T(8,128)}, u32[]{:S(2)}) copy-start(f32[128,768]{1,0:T(8,128)} %all-reduce.3.cloned.1.call-done) | copy-start | bytes 1179652
Sparse Core Ops, SparseCore 0:
  9.0 63.2 all-gather.4
  141.9 30.5 reduce-scatter.2
  174.8 47.9 all-gather.6
  225.9 102.4 all-reduce.2
  330.5 40.2 all-gather.8
  389.7 24.8 reduce-scatter.4
  416.9 48.0 all-gather.10
